TPU v7x, 32 devices: a whole 2x2x4 slice. The times are simulated.
32 devices in a mesh: groups: 2 (over y), ep: 16 (over z, x, core).
Axes of the slice: x: 2, y: 2, z: 4, core: 2. Of those that a mesh axis runs over, the one named last changes fastest.
Arguments:
- queries: bfloat16 [64, 128, 576], P(('groups', 'ep')), parts along dimension 0, may hold values from -120 to 120
- kv_cache: bfloat16 [64, 256, 576], P(('groups', 'ep')), parts along dimension 0, may hold values from -6 to 6
- kv_lengths: int32 [64], P(('groups', 'ep')), parts along dimension 0, may hold values from 32 to 256, as said below
- moe_input: bfloat16 [64, 7168], P(('groups', 'ep')), parts along dimension 0, may hold values from -6 to 6
- expert_ids: int32 [64, 8], P(('groups', 'ep')), parts along dimension 0, may hold values from 0 to 15, all different within a row; in each aligned block of 2 rows (0 to 1, 2 to 3, ...) at most 2 rows name the same one
- route_weights: float32 [64, 8], P(('groups', 'ep')), parts along dimension 0, may hold values from 0.1 to 1
- w_gate: bfloat16 [32768, 7168], P('ep'), may hold values from -0.0625 to 0.0625
- w_up: bfloat16 [32768, 7168], P('ep'), may hold values from -0.0625 to 0.0625
- w_down: bfloat16 [32768, 7168], P('ep'), may hold values from -0.125 to 0.125
Outputs:
- attended: bfloat16 [64, 128, 512], P(('groups', 'ep')), parts along dimension 0
- moe_output: bfloat16 [64, 7168], P(('groups', 'ep')), parts along dimension 0
There are 2 independent parts, one for each index of `groups`. A program takes and returns all parts, laid end to end along the dimension named above; an argument that names none is the same for every part. Nothing has to cross between parts.
Inputs may be any that keep to these rules, and one draw needn't show every extreme that they name: `expert_ids`: the 8 ids of a row differ. Among the 2 rows of one device no expert is named more than 2 times, and in every draw some expert is named exactly 2 times by the rows of some device. `kv_lengths`: some request in every draw uses all 256 slots.
All inputs are finite; a program needn't handle non-finite values.
Results may differ from a plain program's by a relative error of at most 0.0085.
Values may be sent and summed in bfloat16 or wider, within the bound.
No kernel may reach another device: no remote copies, remote signals or barrier semaphores. Data moves between devices by JAX's collectives and lax.ppermute only.
A program may use at most 128 MiB of HBM per device.

v0:
```python
import jax
import jax.numpy as jnp
from jax import lax
from jax.experimental import pallas as pl
from jax.experimental.pallas import tpu as pltpu
from jax.sharding import PartitionSpec as P


LAT = 512
EXPERTS = 16
LANES = 128
HIDDEN_TILE = 512
COLUMN_TILE = 1024
SLOTS = 4
EXPERT_VMEM = 38 << 20

score_scale = 192.0 ** (-0.5)
rows_by_rows = (((1,), (1,)), ((), ()))


def attend_latent(queries, kv_cache, kv_lengths):
    scores = (
        jnp.einsum("rhk,rlk->rhl", queries, kv_cache, preferred_element_type=jnp.float32)
        * score_scale
    )
    slot_index = lax.broadcasted_iota(jnp.int32, scores.shape, 2)
    usable = slot_index < kv_lengths[:, None, None]
    scores = jnp.where(usable, scores, -1e30)
    row_max = jnp.max(scores, axis=2, keepdims=True)
    raw_weights = jnp.where(usable, jnp.exp(scores - row_max), 0.0)
    probs = (raw_weights / jnp.sum(raw_weights, axis=2, keepdims=True)).astype(jnp.bfloat16)
    values = kv_cache[:, :, :LAT]
    return jnp.einsum("rhl,rlk->rhk", probs, values, preferred_element_type=jnp.float32).astype(
        jnp.bfloat16
    )


def largest_tile(size, unit, most):
    return max(t for t in range(unit, min(size, most) + 1, unit) if size % t == 0)


def pack_kernel(inputs, ids, weights, out_ref, inputs_ref, ids_ref, weights_ref, sem):
    requests, width = inputs_ref.shape
    pairs = ((ids, ids_ref), (weights, weights_ref), (inputs, inputs_ref))
    copies = [
        pltpu.make_async_copy(source, target, sem.at[i])
        for i, (source, target) in enumerate(pairs)
    ]
    for copy in copies:
        copy.start()
    for copy in copies:
        copy.wait()
    out_ref[:, pl.ds(0, width)] = inputs_ref[...]
    lane = lax.broadcasted_iota(jnp.int32, (requests, LANES), 1)
    expert = jnp.where(lane < EXPERTS, lane, lane - EXPERTS)
    dense = jnp.zeros((requests, LANES), jnp.float32)
    for route in range(ids_ref.shape[1]):
        named = expert == ids_ref[:, route : route + 1]
        dense = dense + jnp.where(named, weights_ref[:, route : route + 1], 0.0)
    high = dense.astype(out_ref.dtype).astype(jnp.float32)
    low = jnp.where(lane < 2 * EXPERTS, dense - high, 0.0)
    parts = jnp.where(lane < EXPERTS, high, low)
    out_ref[:, pl.ds(width, LANES)] = parts.astype(out_ref.dtype)


def pack(moe_input, expert_ids, route_weights):
    requests, width = moe_input.shape
    operands = (moe_input, expert_ids, route_weights)
    return pl.pallas_call(
        pack_kernel,
        out_shape=jax.ShapeDtypeStruct((requests, width + LANES), moe_input.dtype),
        in_specs=[pl.BlockSpec(memory_space=pltpu.HBM)] * 3,
        out_specs=pl.BlockSpec(memory_space=pltpu.VMEM),
        scratch_shapes=[pltpu.VMEM(operand.shape, operand.dtype) for operand in operands]
        + [pltpu.SemaphoreType.DMA((3,))],
        compiler_params=pltpu.CompilerParams(vmem_limit_bytes=8 << 20),
        cost_estimate=pl.CostEstimate(
            flops=0, bytes_accessed=4 * requests * width, transcendentals=0
        ),
        name="pack",
    )(*(pltpu.with_memory_space_constraint(operand, pltpu.HBM) for operand in operands))


def preload_kernel(expert_ref, source, target, sem):
    copy = pltpu.make_async_copy(source.at[pl.ds(0, target.shape[0]), :], target, sem)
    copy.start()
    copy.wait()


def preload(expert, source, tile):
    width = source.shape[1]
    return pl.pallas_call(
        preload_kernel,
        out_shape=jax.ShapeDtypeStruct((tile, width), source.dtype),
        in_specs=[pl.BlockSpec(memory_space=pltpu.SMEM), pl.BlockSpec(memory_space=pltpu.HBM)],
        out_specs=pl.BlockSpec(memory_space=pltpu.VMEM),
        scratch_shapes=[pltpu.SemaphoreType.DMA],
        compiler_params=pltpu.CompilerParams(vmem_limit_bytes=40 << 20),
        cost_estimate=pl.CostEstimate(
            flops=0, bytes_accessed=2 * tile * width, transcendentals=0
        ),
        name="preload",
    )(expert, source)


def join_kernel(own_ref, other_ref, out_ref):
    half = own_ref.shape[0]
    out_ref[pl.ds(0, half), :] = own_ref[...]
    out_ref[pl.ds(half, half), :] = other_ref[...]


def join(own, other):
    half, width = own.shape
    in_vmem = pl.BlockSpec(memory_space=pltpu.VMEM)
    return pl.pallas_call(
        join_kernel,
        out_shape=jax.ShapeDtypeStruct((2 * half, width), own.dtype),
        in_specs=[in_vmem, in_vmem],
        out_specs=in_vmem,
        compiler_params=pltpu.CompilerParams(vmem_limit_bytes=16 << 20),
        cost_estimate=pl.CostEstimate(
            flops=0, bytes_accessed=8 * half * width, transcendentals=0
        ),
        name="join",
    )(own, other)


def expert_kernel(expert_ref, own_ref, other_ref, *refs):
    first_gate, first_up, w_gate, w_up, w_down, keep_ref, send_ref = refs[:7]
    tokens, gate_act, hid, total, buf, sem = refs[7:]
    half, width = keep_ref.shape
    slots, tile, _ = buf.shape
    sources = (w_gate, w_up, w_down)
    loaded = (first_gate, first_up)
    tiles = w_down.shape[0] // tile
    items = len(sources) * tiles
    columns = largest_tile(width, LANES, COLUMN_TILE)

    def fetch(item):
        kind, slot = item % len(sources), item % slots
        source = sources[kind].at[pl.ds((item // len(sources)) * tile, tile), :]
        return pltpu.make_async_copy(source, buf.at[slot], sem.at[slot])

    for item in range(len(loaded), min(len(loaded) + slots, items)):
        fetch(item).start()
    tokens[pl.ds(0, half), :] = own_ref[...]
    tokens[pl.ds(half, half), :] = other_ref[...]

    extra = tokens[:, pl.ds(width, LANES)].astype(jnp.float32)
    lane = lax.broadcasted_iota(jnp.int32, extra.shape, 1)
    expert = expert_ref[0]
    mine = (lane == expert) | (lane == expert + EXPERTS)
    scale = jnp.sum(jnp.where(mine, extra, 0.0), axis=1, keepdims=True)

    for item in range(items):
        if item >= len(loaded):
            fetch(item).wait()
        weights = loaded[item] if item < len(loaded) else buf.at[item % slots]
        kind, index = item % len(sources), item // len(sources)
        if kind < 2:
            act = lax.dot_general(
                tokens[:, pl.ds(0, width)],
                weights[...],
                rows_by_rows,
                preferred_element_type=jnp.float32,
            )
            if kind == 0:
                gate_act[...] = act
            else:
                gated = gate_act[...]
                hid[...] = (gated / (1.0 + jnp.exp(-gated)) * act).astype(hid.dtype)
        else:
            for start in range(0, width, columns):
                where = pl.ds(start, columns)
                partial = jnp.dot(
                    hid[...], weights[:, where], preferred_element_type=jnp.float32
                )
                if index > 0:
                    partial = partial + total[:, where]
                if index < tiles - 1:
                    total[:, where] = partial
                else:
                    partial = partial * scale
                    keep_ref[:, where] = partial[:half]
                    send_ref[:, where] = partial[half:].astype(send_ref.dtype)
        if item >= len(loaded) and item + slots < items:
            fetch(item + slots).start()


def run_expert(expert, own, other, loaded, w_gate, w_up, w_down):
    half = own.shape[0]
    hidden, width = w_down.shape
    tile = loaded[0].shape[0]
    in_vmem = pl.BlockSpec(memory_space=pltpu.VMEM)
    in_place = pl.BlockSpec(memory_space=pltpu.HBM)
    return pl.pallas_call(
        expert_kernel,
        out_shape=(
            jax.ShapeDtypeStruct((half, width), jnp.float32),
            jax.ShapeDtypeStruct((half, width), own.dtype),
        ),
        in_specs=[pl.BlockSpec(memory_space=pltpu.SMEM)] + [in_vmem] * 4 + [in_place] * 3,
        out_specs=(in_vmem, in_vmem),
        scratch_shapes=[
            pltpu.VMEM((2 * half, own.shape[1]), own.dtype),
            pltpu.VMEM((2 * half, tile), jnp.float32),
            pltpu.VMEM((2 * half, tile), own.dtype),
            pltpu.VMEM((2 * half, width), jnp.float32),
            pltpu.VMEM((SLOTS, tile, width), w_gate.dtype),
            pltpu.SemaphoreType.DMA((SLOTS,)),
        ],
        compiler_params=pltpu.CompilerParams(vmem_limit_bytes=EXPERT_VMEM),
        cost_estimate=pl.CostEstimate(
            flops=12 * half * hidden * width,
            bytes_accessed=6 * hidden * width,
            transcendentals=2 * half * hidden,
        ),
        name="expert",
    )(expert, own, other, *loaded, w_gate, w_up, w_down)


def swap(value, mask, devices):
    return lax.ppermute(value, "ep", [(i, i ^ mask) for i in range(devices)])


def layer(
    queries, kv_cache, kv_lengths, moe_input, expert_ids, route_weights, w_gate, w_up, w_down
):
    attended = attend_latent(queries, kv_cache, kv_lengths)
    devices = lax.axis_size("ep")
    slices = devices // EXPERTS

    rows = pack(moe_input, expert_ids, route_weights)
    expert = (lax.axis_index("ep") // slices).astype(jnp.int32).reshape(1)
    tile = largest_tile(w_gate.shape[0], LANES, HIDDEN_TILE)
    first_gate = preload(expert, w_gate, tile)
    first_up = preload(expert, w_up, tile)
    loaded = (first_gate, first_up)

    masks = [1 << bit for bit in range(devices.bit_length() - 1)]
    for mask in reversed(masks[1:]):
        arrived = swap(rows, mask, devices)
        if mask in masks[1:3]:
            rows = join(rows, arrived)
        else:
            rows = jnp.concatenate([rows, arrived], axis=0)
    other = swap(rows, masks[0], devices)

    keep, send = run_expert(expert, rows, other, loaded, w_gate, w_up, w_down)
    total = keep + swap(send, masks[0], devices).astype(jnp.float32)
    for mask in masks[1:]:
        half = total.shape[0] // 2
        arrived = swap(total[half:].astype(moe_input.dtype), mask, devices)
        total = total[:half] + arrived.astype(jnp.float32)
    return (attended, total.astype(jnp.bfloat16))


def solution(mesh):
    in_specs = (
        P(("groups", "ep"), None, None),
        P(("groups", "ep"), None, None),
        P(("groups", "ep")),
        P(("groups", "ep"), None),
        P(("groups", "ep"), None),
        P(("groups", "ep"), None),
        P("ep", None),
        P("ep", None),
        P("ep", None),
    )
    out_specs = (P(("groups", "ep"), None, None), P(("groups", "ep"), None))
    return jax.shard_map(layer, mesh=mesh, in_specs=in_specs, out_specs=out_specs, check_vma=False)
```

profile of v0, /device:TPU:0, one launch (start us, length us, event | category | flops | bytes accessed | tf_op | source)
XLA Modules:
  0.0 68.9 jit_solution(3977356931730870332)
XLA Ops:
  0.6 0.0 copy-start
  0.6 0.9 %pack.1 = bf16[2,7296]{1,0:T(2,128)(2,1)S(1)} custom-call(bf16[2,7168]{1,0:T(2,128)(2,1)} %inputs.1, s32[2,8]{1,0:T(2,128)} %ids.1, f32[2,8]{1,0:T(2,128)} %weights.1), custom_call_target="tpu_custom_call" | custom-call | bytes 57344 | tf_op jit(solution)/shard_map/pack/pallas_call | solution.py:69
  1.6 4.1 %collective-permute-start = (bf16[2,7296]{1,0:T(2,128)(2,1)S(1)}, bf16[2,7296]{1,0:T(2,128)(2,1)S(1)}, u32[]{:S(2)}, u32[]{:S(2)}) collective-permute-start(bf16[2,7296]{1,0:T(2,128)(2,1)S(1)} %pack.1), channel_id=1, source_target_pairs={{0,8},{1,9},{2,10},{3,11},{4,12},{5,13},{6,14},{7,15},{8,0},{9,1},... | collective-permute-start | bytes 87560 | tf_op jit(solution)/shard_map/ppermute | solution.py:223
  5.7 2.2 %collective-permute-done = bf16[2,7296]{1,0:T(2,128)(2,1)S(1)} collective-permute-done((bf16[2,7296]{1,0:T(2,128)(2,1)S(1)}, bf16[2,7296]{1,0:T(2,128)(2,1)S(1)}, u32[]{:S(2)}, u32[]{:S(2)}) %collective-permute-start) | collective-permute-done | bytes 29216 | tf_op jit(solution)/shard_map/ppermute | solution.py:223
  7.9 0.1 pad_maximum_fusion.own_ref
  8.0 1.7 %collective-permute-start.1 = (bf16[4,7296]{1,0:T(4,128)(2,1)S(1)}, bf16[4,7296]{1,0:T(4,128)(2,1)S(1)}, u32[]{:S(2)}, u32[]{:S(2)}) collective-permute-start(bf16[4,7296]{1,0:T(4,128)(2,1)S(1)} %pad_maximum_fusion.own_ref), channel_id=1, source_target_pairs={{0,4},{1,5},{2,6},{3,7},{4,0},{5,1},{6,2},{7,3},{8,12},{9,13},{10,... | collective-permute-start | bytes 175112 | tf_op jit(solution)/shard_map/ppermute | solution.py:223
  9.6 2.6 %collective-permute-done.1.other_ref = bf16[4,7296]{1,0:T(4,128)(2,1)S(1)} collective-permute-done((bf16[4,7296]{1,0:T(4,128)(2,1)S(1)}, bf16[4,7296]{1,0:T(4,128)(2,1)S(1)}, u32[]{:S(2)}, u32[]{:S(2)}) %collective-permute-start.1) | collective-permute-done | bytes 58400 | tf_op jit(solution)/shard_map/ppermute | solution.py:223
  12.3 1.8 %collective-permute-start.2 = (bf16[8,7296]{1,0:T(8,128)(2,1)S(1)}, bf16[8,7296]{1,0:T(8,128)(2,1)S(1)}, u32[]{:S(2)}, u32[]{:S(2)}) collective-permute-start(bf16[8,7296]{1,0:T(8,128)(2,1)S(1)} %join.2.own_ref), channel_id=1, source_target_pairs={{0,2},{1,3},{2,0},{3,1},{4,6},{5,7},{6,4},{7,5},{8,10},{9,11},{10,... | collective-permute-start | bytes 350216 | tf_op jit(solution)/shard_map/ppermute | solution.py:223
  14.0 3.1 %collective-permute-done.2.other_ref = bf16[8,7296]{1,0:T(8,128)(2,1)S(1)} collective-permute-done((bf16[8,7296]{1,0:T(8,128)(2,1)S(1)}, bf16[8,7296]{1,0:T(8,128)(2,1)S(1)}, u32[]{:S(2)}, u32[]{:S(2)}) %collective-permute-start.2) | collective-permute-done | bytes 116768 | tf_op jit(solution)/shard_map/ppermute | solution.py:223
  17.2 0.1 collective-permute-start.3
  17.2 3.1 %preload.2.refs_0_ = bf16[512,7168]{1,0:T(8,128)(2,1)S(1)} custom-call(s32[1]{0:T(128)} %bitcast.expert_ref, bf16[2048,7168]{1,0:T(8,128)(2,1)} %refs_2_.1), custom_call_target="tpu_custom_call" | custom-call | bytes 7340032 | tf_op jit(solution)/shard_map/preload/pallas_call | solution.py:92
  20.3 3.1 %preload.3.refs_1_ = bf16[512,7168]{1,0:T(8,128)(2,1)S(1)} custom-call(s32[1]{0:T(128)} %bitcast.expert_ref, bf16[2048,7168]{1,0:T(8,128)(2,1)} %refs_3_.1), custom_call_target="tpu_custom_call" | custom-call | bytes 7340032 | tf_op jit(solution)/shard_map/preload/pallas_call | solution.py:92
  23.4 0.0 copy-start.1
  23.5 0.0 copy-start.2
  23.5 0.0 collective-permute-done.3.other_ref
  23.5 28.3 %expert.1 = (f32[16,7168]{1,0:T(8,128)S(1)}, bf16[16,7168]{1,0:T(8,128)(2,1)S(1)}) custom-call(s32[1]{0:T(128)} %bitcast.expert_ref, bf16[16,7296]{1,0:T(8,128)(2,1)S(1)} %join.3.own_ref, bf16[16,7296]{1,0:T(8,128)(2,1)S(1)} %collective-permute-done.3.other_ref, bf16[512,7168]{1,0:T(8,128)(2,1)S(1)} %preload.2.refs_0_, ...), custom_call_target="tpu_custom_call" | custom-call | flops 2818572288 | bytes 88080384 | tf_op jit(solution)/shard_map/expert/pallas_call | solution.py:196
  51.8 0.6 collective-permute-start.4
  52.4 1.1 %collective-permute-done.4 = bf16[16,7168]{1,0:T(8,128)(2,1)S(1)} collective-permute-done((bf16[16,7168]{1,0:T(8,128)(2,1)S(1)}, bf16[16,7168]{1,0:T(8,128)(2,1)S(1)}, u32[]{:S(2)}, u32[]{:S(2)}) %collective-permute-start.4) | collective-permute-done | bytes 229408 | tf_op jit(solution)/shard_map/ppermute | solution.py:223
  53.6 1.8 %collective-permute-start.5 = (bf16[8,7168]{1,0:T(8,128)(2,1)S(1)}, bf16[8,7168]{1,0:T(8,128)(2,1)S(1)}, u32[]{:S(2)}, u32[]{:S(2)}) collective-permute-start(bf16[8,7168]{1,0:T(8,128)(2,1)S(1)} %slice.47), channel_id=1, source_target_pairs={{0,2},{1,3},{2,0},{3,1},{4,6},{5,7},{6,4},{7,5},{8,10},{9,11},{10,... | collective-permute-start | bytes 344072 | tf_op jit(solution)/shard_map/ppermute | solution.py:223
  55.3 0.0 copy-done
  55.3 0.0 copy-done.1
  55.3 0.0 copy-done.2
  55.3 0.3 fusion.4
  55.7 3.4 %collective-permute-done.5 = bf16[8,7168]{1,0:T(8,128)(2,1)S(1)} collective-permute-done((bf16[8,7168]{1,0:T(8,128)(2,1)S(1)}, bf16[8,7168]{1,0:T(8,128)(2,1)S(1)}, u32[]{:S(2)}, u32[]{:S(2)}) %collective-permute-start.5) | collective-permute-done | bytes 114720 | tf_op jit(solution)/shard_map/ppermute | solution.py:223
  59.1 1.7 %collective-permute-start.6 = (bf16[4,7168]{1,0:T(4,128)(2,1)S(1)}, bf16[4,7168]{1,0:T(4,128)(2,1)S(1)}, u32[]{:S(2)}, u32[]{:S(2)}) collective-permute-start(bf16[4,7168]{1,0:T(4,128)(2,1)S(1)} %slice.48), channel_id=1, source_target_pairs={{0,4},{1,5},{2,6},{3,7},{4,0},{5,1},{6,2},{7,3},{8,12},{9,13},{10,... | collective-permute-start | bytes 172040 | tf_op jit(solution)/shard_map/ppermute | solution.py:223
  60.8 0.2 fusion.10
  61.0 2.4 %collective-permute-done.6 = bf16[4,7168]{1,0:T(4,128)(2,1)S(1)} collective-permute-done((bf16[4,7168]{1,0:T(4,128)(2,1)S(1)}, bf16[4,7168]{1,0:T(4,128)(2,1)S(1)}, u32[]{:S(2)}, u32[]{:S(2)}) %collective-permute-start.6) | collective-permute-done | bytes 57376 | tf_op jit(solution)/shard_map/ppermute | solution.py:223
  63.4 2.7 %collective-permute-start.7 = (bf16[2,7168]{1,0:T(2,128)(2,1)S(1)}, bf16[2,7168]{1,0:T(2,128)(2,1)S(1)}, u32[]{:S(2)}, u32[]{:S(2)}) collective-permute-start(bf16[2,7168]{1,0:T(2,128)(2,1)S(1)} %slice.49), channel_id=1, source_target_pairs={{0,8},{1,9},{2,10},{3,11},{4,12},{5,13},{6,14},{7,15},{8,0},{9,1},... | collective-permute-start | bytes 86024 | tf_op jit(solution)/shard_map/ppermute | solution.py:223
  66.1 1.2 %convolution_convert_fusion = bf16[2,128,512]{2,1,0:T(8,128)(2,1)} fusion(bf16[2,256,576]{1,2,0:T(8,128)(2,1)S(1)} %copy-done.1, f32[2,128]{1,0:T(2,128)S(1)} %fusion.10, f32[2,128,256]{2,1,0:T(8,128)S(1)} %fusion.4, s32[2]{0:T(128)S(1)} %copy-done.2), kind=kOutput, calls=%fused_computation.2 | convolution fusion | flops 67568128 | bytes 1312256 | tf_op jit(solution)/shard_map/rhl,rlk->rhk/dot_general | solution.py:33
  67.4 0.9 %collective-permute-done.7 = bf16[2,7168]{1,0:T(2,128)(2,1)S(1)} collective-permute-done((bf16[2,7168]{1,0:T(2,128)(2,1)S(1)}, bf16[2,7168]{1,0:T(2,128)(2,1)S(1)}, u32[]{:S(2)}, u32[]{:S(2)}) %collective-permute-start.7) | collective-permute-done | bytes 28704 | tf_op jit(solution)/shard_map/ppermute | solution.py:223
  68.3 0.6 fusion.7
  (8 shorter events, 0.2 us)
Async XLA Ops:
  0.6 54.7 %copy-start = (bf16[2,128,576]{1,2,0:T(8,128)(2,1)S(1)}, bf16[2,128,576]{1,2,0:T(8,128)(2,1)}, u32[]{:S(2)}) copy-start(bf16[2,128,576]{1,2,0:T(8,128)(2,1)} %param.9) | copy-start | bytes 884740
  1.6 6.3 %collective-permute-start = (bf16[2,7296]{1,0:T(2,128)(2,1)S(1)}, bf16[2,7296]{1,0:T(2,128)(2,1)S(1)}, u32[]{:S(2)}, u32[]{:S(2)}) collective-permute-start(bf16[2,7296]{1,0:T(2,128)(2,1)S(1)} %pack.1), channel_id=1, source_target_pairs={{0,8},{1,9},{2,10},{3,11},{4,12},{5,13},{6,14},{7,15},{8,0},{9,1},... | collective-permute-start | bytes 87560 | tf_op jit(solution)/shard_map/ppermute | solution.py:223
  8.0 4.3 %collective-permute-start.1 = (bf16[4,7296]{1,0:T(4,128)(2,1)S(1)}, bf16[4,7296]{1,0:T(4,128)(2,1)S(1)}, u32[]{:S(2)}, u32[]{:S(2)}) collective-permute-start(bf16[4,7296]{1,0:T(4,128)(2,1)S(1)} %pad_maximum_fusion.own_ref), channel_id=1, source_target_pairs={{0,4},{1,5},{2,6},{3,7},{4,0},{5,1},{6,2},{7,3},{8,12},{9,13},{10,... | collective-permute-start | bytes 175112 | tf_op jit(solution)/shard_map/ppermute | solution.py:223
  12.3 4.9 %collective-permute-start.2 = (bf16[8,7296]{1,0:T(8,128)(2,1)S(1)}, bf16[8,7296]{1,0:T(8,128)(2,1)S(1)}, u32[]{:S(2)}, u32[]{:S(2)}) collective-permute-start(bf16[8,7296]{1,0:T(8,128)(2,1)S(1)} %join.2.own_ref), channel_id=1, source_target_pairs={{0,2},{1,3},{2,0},{3,1},{4,6},{5,7},{6,4},{7,5},{8,10},{9,11},{10,... | collective-permute-start | bytes 350216 | tf_op jit(solution)/shard_map/ppermute | solution.py:223
  17.2 6.3 %collective-permute-start.3 = (bf16[16,7296]{1,0:T(8,128)(2,1)S(1)}, bf16[16,7296]{1,0:T(8,128)(2,1)S(1)}, u32[]{:S(2)}, u32[]{:S(2)}) collective-permute-start(bf16[16,7296]{1,0:T(8,128)(2,1)S(1)} %join.3.own_ref), channel_id=1, source_target_pairs={{0,1},{1,0},{2,3},{3,2},{4,5},{5,4},{6,7},{7,6},{8,9},{9,8},{10,11... | collective-permute-start | bytes 700424 | tf_op jit(solution)/shard_map/ppermute | solution.py:223
  23.4 31.9 %copy-start.1 = (bf16[2,256,576]{1,2,0:T(8,128)(2,1)S(1)}, bf16[2,256,576]{1,2,0:T(8,128)(2,1)}, u32[]{:S(2)}) copy-start(bf16[2,256,576]{1,2,0:T(8,128)(2,1)} %param.10) | copy-start | bytes 1769476
  23.5 31.9 %copy-start.2 = (s32[2]{0:T(128)S(1)}, s32[2]{0:T(128)}, u32[]{:S(2)}) copy-start(s32[2]{0:T(128)} %param.11) | copy-start | bytes 28
  51.8 1.7 %collective-permute-start.4 = (bf16[16,7168]{1,0:T(8,128)(2,1)S(1)}, bf16[16,7168]{1,0:T(8,128)(2,1)S(1)}, u32[]{:S(2)}, u32[]{:S(2)}) collective-permute-start(bf16[16,7168]{1,0:T(8,128)(2,1)S(1)} %get-tuple-element.5), channel_id=1, source_target_pairs={{0,1},{1,0},{2,3},{3,2},{4,5},{5,4},{6,7},{7,6},{8,9},{9,8},{10,11... | collective-permute-start | bytes 688136 | tf_op jit(solution)/shard_map/ppermute | solution.py:223
  53.6 5.5 %collective-permute-start.5 = (bf16[8,7168]{1,0:T(8,128)(2,1)S(1)}, bf16[8,7168]{1,0:T(8,128)(2,1)S(1)}, u32[]{:S(2)}, u32[]{:S(2)}) collective-permute-start(bf16[8,7168]{1,0:T(8,128)(2,1)S(1)} %slice.47), channel_id=1, source_target_pairs={{0,2},{1,3},{2,0},{3,1},{4,6},{5,7},{6,4},{7,5},{8,10},{9,11},{10,... | collective-permute-start | bytes 344072 | tf_op jit(solution)/shard_map/ppermute | solution.py:223
  59.1 4.2 %collective-permute-start.6 = (bf16[4,7168]{1,0:T(4,128)(2,1)S(1)}, bf16[4,7168]{1,0:T(4,128)(2,1)S(1)}, u32[]{:S(2)}, u32[]{:S(2)}) collective-permute-start(bf16[4,7168]{1,0:T(4,128)(2,1)S(1)} %slice.48), channel_id=1, source_target_pairs={{0,4},{1,5},{2,6},{3,7},{4,0},{5,1},{6,2},{7,3},{8,12},{9,13},{10,... | collective-permute-start | bytes 172040 | tf_op jit(solution)/shard_map/ppermute | solution.py:223
  63.4 4.8 %collective-permute-start.7 = (bf16[2,7168]{1,0:T(2,128)(2,1)S(1)}, bf16[2,7168]{1,0:T(2,128)(2,1)S(1)}, u32[]{:S(2)}, u32[]{:S(2)}) collective-permute-start(bf16[2,7168]{1,0:T(2,128)(2,1)S(1)} %slice.49), channel_id=1, source_target_pairs={{0,8},{1,9},{2,10},{3,11},{4,12},{5,13},{6,14},{7,15},{8,0},{9,1},... | collective-permute-start | bytes 86024 | tf_op jit(solution)/shard_map/ppermute | solution.py:223
where the time goes:
time: 69.1 us; the launch traced here: 68.9 us
  Pallas kernels  35.5 us (51%)
  waiting for transfers between devices  15.6 us (23%)
  starting transfers between devices  14.3 us (21%)
  matrix products  1.56 us (2%)
  other arithmetic  1.03 us (1%)
  between operations  0.77 us (1%)
    pallas_call x1, Pallas kernels, run_expert(): pl.pallas_call(expert_kernel, out_shape=(jax.ShapeDtypeStruct((half, widt...  28.3 us
    ppermute x8, waiting for transfers between devices, swap(): return lax.ppermute(value, 'ep', [(i, i ^ mask) for i in range(devices)])  15.6 us
    ppermute x8, starting transfers between devices, swap(): return lax.ppermute(value, 'ep', [(i, i ^ mask) for i in range(devices)])  14.3 us
    pallas_call x2, Pallas kernels, preload(): pl.pallas_call(preload_kernel, out_shape=jax.ShapeDtypeStruct((tile, widt...  6.19 us
  transfers between devices with their start and end apart: 8, of which 7 were waited for; matrix products, arithmetic and copies ran while one was open for 3% of the time, Pallas kernels for 9%

commit v1 on v0

--- a/solution.py
+++ b/solution.py
@@ -1,3 +1,5 @@
+import functools
+
 import jax
 import jax.numpy as jnp
 from jax import lax
@@ -81,16 +83,16 @@
     )(*(pltpu.with_memory_space_constraint(operand, pltpu.HBM) for operand in operands))
 
 
-def preload_kernel(expert_ref, source, target, sem):
-    copy = pltpu.make_async_copy(source.at[pl.ds(0, target.shape[0]), :], target, sem)
+def preload_kernel(start, expert_ref, source, target, sem):
+    copy = pltpu.make_async_copy(source.at[pl.ds(start, target.shape[0]), :], target, sem)
     copy.start()
     copy.wait()
 
 
-def preload(expert, source, tile):
+def preload(expert, source, start, tile):
     width = source.shape[1]
     return pl.pallas_call(
-        preload_kernel,
+        functools.partial(preload_kernel, start),
         out_shape=jax.ShapeDtypeStruct((tile, width), source.dtype),
         in_specs=[pl.BlockSpec(memory_space=pltpu.SMEM), pl.BlockSpec(memory_space=pltpu.HBM)],
         out_specs=pl.BlockSpec(memory_space=pltpu.VMEM),
@@ -126,12 +128,12 @@
 
 
 def expert_kernel(expert_ref, own_ref, other_ref, *refs):
-    first_gate, first_up, w_gate, w_up, w_down, keep_ref, send_ref = refs[:7]
-    tokens, gate_act, hid, total, buf, sem = refs[7:]
+    lower_gate, upper_gate, first_up, w_gate, w_up, w_down, keep_ref, send_ref = refs[:8]
+    tokens, gate_act, hid, total, buf, sem = refs[8:]
     half, width = keep_ref.shape
     slots, tile, _ = buf.shape
     sources = (w_gate, w_up, w_down)
-    loaded = (first_gate, first_up)
+    loaded = ((lower_gate, upper_gate), (first_up,))
     tiles = w_down.shape[0] // tile
     items = len(sources) * tiles
     columns = largest_tile(width, LANES, COLUMN_TILE)
@@ -155,15 +157,20 @@
     for item in range(items):
         if item >= len(loaded):
             fetch(item).wait()
-        weights = loaded[item] if item < len(loaded) else buf.at[item % slots]
+        pieces = loaded[item] if item < len(loaded) else (buf.at[item % slots],)
+        weights = pieces[0]
         kind, index = item % len(sources), item // len(sources)
         if kind < 2:
-            act = lax.dot_general(
-                tokens[:, pl.ds(0, width)],
-                weights[...],
-                rows_by_rows,
-                preferred_element_type=jnp.float32,
-            )
+            acts = [
+                lax.dot_general(
+                    tokens[:, pl.ds(0, width)],
+                    piece[...],
+                    rows_by_rows,
+                    preferred_element_type=jnp.float32,
+                )
+                for piece in pieces
+            ]
+            act = jnp.concatenate(acts, axis=1) if len(acts) > 1 else acts[0]
             if kind == 0:
                 gate_act[...] = act
             else:
@@ -190,7 +197,7 @@
 def run_expert(expert, own, other, loaded, w_gate, w_up, w_down):
     half = own.shape[0]
     hidden, width = w_down.shape
-    tile = loaded[0].shape[0]
+    tile = loaded[-1].shape[0]
     in_vmem = pl.BlockSpec(memory_space=pltpu.VMEM)
     in_place = pl.BlockSpec(memory_space=pltpu.HBM)
     return pl.pallas_call(
@@ -199,7 +206,7 @@
             jax.ShapeDtypeStruct((half, width), jnp.float32),
             jax.ShapeDtypeStruct((half, width), own.dtype),
         ),
-        in_specs=[pl.BlockSpec(memory_space=pltpu.SMEM)] + [in_vmem] * 4 + [in_place] * 3,
+        in_specs=[pl.BlockSpec(memory_space=pltpu.SMEM)] + [in_vmem] * 5 + [in_place] * 3,
         out_specs=(in_vmem, in_vmem),
         scratch_shapes=[
             pltpu.VMEM((2 * half, own.shape[1]), own.dtype),
@@ -233,14 +240,15 @@
     rows = pack(moe_input, expert_ids, route_weights)
     expert = (lax.axis_index("ep") // slices).astype(jnp.int32).reshape(1)
     tile = largest_tile(w_gate.shape[0], LANES, HIDDEN_TILE)
-    first_gate = preload(expert, w_gate, tile)
-    first_up = preload(expert, w_up, tile)
-    loaded = (first_gate, first_up)
+    lower_gate = preload(expert, w_gate, 0, tile // 2)
+    upper_gate = preload(expert, w_gate, tile // 2, tile // 2)
+    first_up = preload(expert, w_up, 0, tile)
+    loaded = (lower_gate, upper_gate, first_up)
 
     masks = [1 << bit for bit in range(devices.bit_length() - 1)]
     for mask in reversed(masks[1:]):
         arrived = swap(rows, mask, devices)
-        if mask in masks[1:3]:
+        if mask in masks[1:4]:
             rows = join(rows, arrived)
         else:
             rows = jnp.concatenate([rows, arrived], axis=0)

time: 69.1 us -> 70.1 us (1.014)
  Pallas kernels: 35.5 us -> 36.6 us
    pallas_call x2 -> x3, Pallas kernels: 6.19 us -> 7.19 us  [preload(): pl.pallas_call(functools.partial(preload_kernel, start), out_shape=jax.Sh...]
  transfers between devices with their start and end apart: 8 -> 8, of which waited for: 7 -> 7; matrix products, arithmetic and copies ran while one was open for 3% -> 3% of each run, Pallas kernels for 9% -> 10%
where the time goes in v1:
time: 70.1 us; the launch traced here: 69.9 us
  Pallas kernels  36.6 us (52%)
  waiting for transfers between devices  15.6 us (22%)
  starting transfers between devices  14.3 us (20%)
  matrix products  1.56 us (2%)
  other arithmetic  0.96 us (1%)
  between operations  0.78 us (1%)
    pallas_call x1, Pallas kernels, run_expert(): pl.pallas_call(expert_kernel, out_shape=(jax.ShapeDtypeStruct((half, widt...  28.4 us
    ppermute x8, waiting for transfers between devices, swap(): return lax.ppermute(value, 'ep', [(i, i ^ mask) for i in range(devices)])  15.6 us
    ppermute x8, starting transfers between devices, swap(): return lax.ppermute(value, 'ep', [(i, i ^ mask) for i in range(devices)])  14.3 us
    pallas_call x3, Pallas kernels, preload(): pl.pallas_call(functools.partial(preload_kernel, start), out_shape=jax.Sh...  7.19 us
  transfers between devices with their start and end apart: 8, of which 7 were waited for; matrix products, arithmetic and copies ran while one was open for 3% of the time, Pallas kernels for 10%

profile of v1, /device:TPU:0, one launch (start us, length us, event | category | flops | bytes accessed | tf_op | source)
XLA Modules:
  0.0 69.9 jit_solution(7516749777618492548)
XLA Ops:
  0.6 0.0 copy-start
  0.6 0.9 %pack.1.own_ref = bf16[2,7296]{1,0:T(2,128)(2,1)S(1)} custom-call(bf16[2,7168]{1,0:T(2,128)(2,1)} %inputs.1, s32[2,8]{1,0:T(2,128)} %ids.1, f32[2,8]{1,0:T(2,128)} %weights.1), custom_call_target="tpu_custom_call" | custom-call | bytes 57344 | tf_op jit(solution)/shard_map/pack/pallas_call | solution.py:71
  1.6 4.1 %collective-permute-start = (bf16[2,7296]{1,0:T(2,128)(2,1)S(1)}, bf16[2,7296]{1,0:T(2,128)(2,1)S(1)}, u32[]{:S(2)}, u32[]{:S(2)}) collective-permute-start(bf16[2,7296]{1,0:T(2,128)(2,1)S(1)} %pack.1.own_ref), channel_id=1, source_target_pairs={{0,8},{1,9},{2,10},{3,11},{4,12},{5,13},{6,14},{7,15},{8,0},{9,1},... | collective-permute-start | bytes 87560 | tf_op jit(solution)/shard_map/ppermute | solution.py:230
  5.7 2.2 %collective-permute-done.other_ref = bf16[2,7296]{1,0:T(2,128)(2,1)S(1)} collective-permute-done((bf16[2,7296]{1,0:T(2,128)(2,1)S(1)}, bf16[2,7296]{1,0:T(2,128)(2,1)S(1)}, u32[]{:S(2)}, u32[]{:S(2)}) %collective-permute-start) | collective-permute-done | bytes 29216 | tf_op jit(solution)/shard_map/ppermute | solution.py:230
  7.9 1.7 %collective-permute-start.1 = (bf16[4,7296]{1,0:T(4,128)(2,1)S(1)}, bf16[4,7296]{1,0:T(4,128)(2,1)S(1)}, u32[]{:S(2)}, u32[]{:S(2)}) collective-permute-start(bf16[4,7296]{1,0:T(4,128)(2,1)S(1)} %join.3.own_ref), channel_id=1, source_target_pairs={{0,4},{1,5},{2,6},{3,7},{4,0},{5,1},{6,2},{7,3},{8,12},{9,13},{10,... | collective-permute-start | bytes 175112 | tf_op jit(solution)/shard_map/ppermute | solution.py:230
  9.6 2.6 %collective-permute-done.1.other_ref = bf16[4,7296]{1,0:T(4,128)(2,1)S(1)} collective-permute-done((bf16[4,7296]{1,0:T(4,128)(2,1)S(1)}, bf16[4,7296]{1,0:T(4,128)(2,1)S(1)}, u32[]{:S(2)}, u32[]{:S(2)}) %collective-permute-start.1) | collective-permute-done | bytes 58400 | tf_op jit(solution)/shard_map/ppermute | solution.py:230
  12.2 1.8 %collective-permute-start.2 = (bf16[8,7296]{1,0:T(8,128)(2,1)S(1)}, bf16[8,7296]{1,0:T(8,128)(2,1)S(1)}, u32[]{:S(2)}, u32[]{:S(2)}) collective-permute-start(bf16[8,7296]{1,0:T(8,128)(2,1)S(1)} %join.4.own_ref), channel_id=1, source_target_pairs={{0,2},{1,3},{2,0},{3,1},{4,6},{5,7},{6,4},{7,5},{8,10},{9,11},{10,... | collective-permute-start | bytes 350216 | tf_op jit(solution)/shard_map/ppermute | solution.py:230
  14.0 3.1 %collective-permute-done.2.other_ref = bf16[8,7296]{1,0:T(8,128)(2,1)S(1)} collective-permute-done((bf16[8,7296]{1,0:T(8,128)(2,1)S(1)}, bf16[8,7296]{1,0:T(8,128)(2,1)S(1)}, u32[]{:S(2)}, u32[]{:S(2)}) %collective-permute-start.2) | collective-permute-done | bytes 116768 | tf_op jit(solution)/shard_map/ppermute | solution.py:230
  17.1 0.1 collective-permute-start.3
  17.2 2.0 %preload.3.refs_0_ = bf16[256,7168]{1,0:T(8,128)(2,1)S(1)} custom-call(s32[1]{0:T(128)} %bitcast.expert_ref, bf16[2048,7168]{1,0:T(8,128)(2,1)} %refs_3_.1), custom_call_target="tpu_custom_call" | custom-call | bytes 3670016 | tf_op jit(solution)/shard_map/preload/pallas_call | solution.py:94
  19.3 2.0 %preload.4.refs_1_ = bf16[256,7168]{1,0:T(8,128)(2,1)S(1)} custom-call(s32[1]{0:T(128)} %bitcast.expert_ref, bf16[2048,7168]{1,0:T(8,128)(2,1)} %refs_3_.1), custom_call_target="tpu_custom_call" | custom-call | bytes 3670016 | tf_op jit(solution)/shard_map/preload/pallas_call | solution.py:94
  21.3 3.1 %preload.5.refs_2_ = bf16[512,7168]{1,0:T(8,128)(2,1)S(1)} custom-call(s32[1]{0:T(128)} %bitcast.expert_ref, bf16[2048,7168]{1,0:T(8,128)(2,1)} %refs_4_.1), custom_call_target="tpu_custom_call" | custom-call | bytes 7340032 | tf_op jit(solution)/shard_map/preload/pallas_call | solution.py:94
  24.4 0.0 copy-start.1
  24.4 0.0 copy-start.2
  24.4 0.0 collective-permute-done.3.other_ref
  24.4 28.4 %expert.1 = (f32[16,7168]{1,0:T(8,128)S(1)}, bf16[16,7168]{1,0:T(8,128)(2,1)S(1)}) custom-call(s32[1]{0:T(128)} %bitcast.expert_ref, bf16[16,7296]{1,0:T(8,128)(2,1)S(1)} %join.5.own_ref, bf16[16,7296]{1,0:T(8,128)(2,1)S(1)} %collective-permute-done.3.other_ref, bf16[256,7168]{1,0:T(8,128)(2,1)S(1)} %preload.3.refs_0_, ...), custom_call_target="tpu_custom_call" | custom-call | flops 2818572288 | bytes 88080384 | tf_op jit(solution)/shard_map/expert/pallas_call | solution.py:203
  52.8 0.6 collective-permute-start.4
  53.4 1.1 %collective-permute-done.4 = bf16[16,7168]{1,0:T(8,128)(2,1)S(1)} collective-permute-done((bf16[16,7168]{1,0:T(8,128)(2,1)S(1)}, bf16[16,7168]{1,0:T(8,128)(2,1)S(1)}, u32[]{:S(2)}, u32[]{:S(2)}) %collective-permute-start.4) | collective-permute-done | bytes 229408 | tf_op jit(solution)/shard_map/ppermute | solution.py:230
  54.5 1.8 %collective-permute-start.5 = (bf16[8,7168]{1,0:T(8,128)(2,1)S(1)}, bf16[8,7168]{1,0:T(8,128)(2,1)S(1)}, u32[]{:S(2)}, u32[]{:S(2)}) collective-permute-start(bf16[8,7168]{1,0:T(8,128)(2,1)S(1)} %slice.47), channel_id=1, source_target_pairs={{0,2},{1,3},{2,0},{3,1},{4,6},{5,7},{6,4},{7,5},{8,10},{9,11},{10,... | collective-permute-start | bytes 344072 | tf_op jit(solution)/shard_map/ppermute | solution.py:230
  56.3 0.0 copy-done
  56.3 0.0 copy-done.1
  56.3 0.0 copy-done.2
  56.3 0.3 fusion.4
  56.6 3.4 %collective-permute-done.5 = bf16[8,7168]{1,0:T(8,128)(2,1)S(1)} collective-permute-done((bf16[8,7168]{1,0:T(8,128)(2,1)S(1)}, bf16[8,7168]{1,0:T(8,128)(2,1)S(1)}, u32[]{:S(2)}, u32[]{:S(2)}) %collective-permute-start.5) | collective-permute-done | bytes 114720 | tf_op jit(solution)/shard_map/ppermute | solution.py:230
  60.1 1.7 %collective-permute-start.6 = (bf16[4,7168]{1,0:T(4,128)(2,1)S(1)}, bf16[4,7168]{1,0:T(4,128)(2,1)S(1)}, u32[]{:S(2)}, u32[]{:S(2)}) collective-permute-start(bf16[4,7168]{1,0:T(4,128)(2,1)S(1)} %slice.48), channel_id=1, source_target_pairs={{0,4},{1,5},{2,6},{3,7},{4,0},{5,1},{6,2},{7,3},{8,12},{9,13},{10,... | collective-permute-start | bytes 172040 | tf_op jit(solution)/shard_map/ppermute | solution.py:230
  61.8 0.2 fusion.10
  62.0 2.4 %collective-permute-done.6 = bf16[4,7168]{1,0:T(4,128)(2,1)S(1)} collective-permute-done((bf16[4,7168]{1,0:T(4,128)(2,1)S(1)}, bf16[4,7168]{1,0:T(4,128)(2,1)S(1)}, u32[]{:S(2)}, u32[]{:S(2)}) %collective-permute-start.6) | collective-permute-done | bytes 57376 | tf_op jit(solution)/shard_map/ppermute | solution.py:230
  64.4 2.7 %collective-permute-start.7 = (bf16[2,7168]{1,0:T(2,128)(2,1)S(1)}, bf16[2,7168]{1,0:T(2,128)(2,1)S(1)}, u32[]{:S(2)}, u32[]{:S(2)}) collective-permute-start(bf16[2,7168]{1,0:T(2,128)(2,1)S(1)} %slice.49), channel_id=1, source_target_pairs={{0,8},{1,9},{2,10},{3,11},{4,12},{5,13},{6,14},{7,15},{8,0},{9,1},... | collective-permute-start | bytes 86024 | tf_op jit(solution)/shard_map/ppermute | solution.py:230
  67.1 1.2 %convolution_convert_fusion = bf16[2,128,512]{2,1,0:T(8,128)(2,1)} fusion(bf16[2,256,576]{1,2,0:T(8,128)(2,1)S(1)} %copy-done.1, f32[2,128]{1,0:T(2,128)S(1)} %fusion.10, f32[2,128,256]{2,1,0:T(8,128)S(1)} %fusion.4, s32[2]{0:T(128)S(1)} %copy-done.2), kind=kOutput, calls=%fused_computation.2 | convolution fusion | flops 67568128 | bytes 1312256 | tf_op jit(solution)/shard_map/rhl,rlk->rhk/dot_general | solution.py:35
  68.3 0.9 %collective-permute-done.7 = bf16[2,7168]{1,0:T(2,128)(2,1)S(1)} collective-permute-done((bf16[2,7168]{1,0:T(2,128)(2,1)S(1)}, bf16[2,7168]{1,0:T(2,128)(2,1)S(1)}, u32[]{:S(2)}, u32[]{:S(2)}) %collective-permute-start.7) | collective-permute-done | bytes 28704 | tf_op jit(solution)/shard_map/ppermute | solution.py:230
  69.2 0.6 fusion.7
  (9 shorter events, 0.2 us)
Async XLA Ops:
  0.6 55.7 %copy-start = (bf16[2,128,576]{1,2,0:T(8,128)(2,1)S(1)}, bf16[2,128,576]{1,2,0:T(8,128)(2,1)}, u32[]{:S(2)}) copy-start(bf16[2,128,576]{1,2,0:T(8,128)(2,1)} %param.9) | copy-start | bytes 884740
  1.6 6.3 %collective-permute-start = (bf16[2,7296]{1,0:T(2,128)(2,1)S(1)}, bf16[2,7296]{1,0:T(2,128)(2,1)S(1)}, u32[]{:S(2)}, u32[]{:S(2)}) collective-permute-start(bf16[2,7296]{1,0:T(2,128)(2,1)S(1)} %pack.1.own_ref), channel_id=1, source_target_pairs={{0,8},{1,9},{2,10},{3,11},{4,12},{5,13},{6,14},{7,15},{8,0},{9,1},... | collective-permute-start | bytes 87560 | tf_op jit(solution)/shard_map/ppermute | solution.py:230
  7.9 4.3 %collective-permute-start.1 = (bf16[4,7296]{1,0:T(4,128)(2,1)S(1)}, bf16[4,7296]{1,0:T(4,128)(2,1)S(1)}, u32[]{:S(2)}, u32[]{:S(2)}) collective-permute-start(bf16[4,7296]{1,0:T(4,128)(2,1)S(1)} %join.3.own_ref), channel_id=1, source_target_pairs={{0,4},{1,5},{2,6},{3,7},{4,0},{5,1},{6,2},{7,3},{8,12},{9,13},{10,... | collective-permute-start | bytes 175112 | tf_op jit(solution)/shard_map/ppermute | solution.py:230
  12.2 4.9 %collective-permute-start.2 = (bf16[8,7296]{1,0:T(8,128)(2,1)S(1)}, bf16[8,7296]{1,0:T(8,128)(2,1)S(1)}, u32[]{:S(2)}, u32[]{:S(2)}) collective-permute-start(bf16[8,7296]{1,0:T(8,128)(2,1)S(1)} %join.4.own_ref), channel_id=1, source_target_pairs={{0,2},{1,3},{2,0},{3,1},{4,6},{5,7},{6,4},{7,5},{8,10},{9,11},{10,... | collective-permute-start | bytes 350216 | tf_op jit(solution)/shard_map/ppermute | solution.py:230
  17.1 7.3 %collective-permute-start.3 = (bf16[16,7296]{1,0:T(8,128)(2,1)S(1)}, bf16[16,7296]{1,0:T(8,128)(2,1)S(1)}, u32[]{:S(2)}, u32[]{:S(2)}) collective-permute-start(bf16[16,7296]{1,0:T(8,128)(2,1)S(1)} %join.5.own_ref), channel_id=1, source_target_pairs={{0,1},{1,0},{2,3},{3,2},{4,5},{5,4},{6,7},{7,6},{8,9},{9,8},{10,11... | collective-permute-start | bytes 700424 | tf_op jit(solution)/shard_map/ppermute | solution.py:230
  24.4 31.9 %copy-start.1 = (bf16[2,256,576]{1,2,0:T(8,128)(2,1)S(1)}, bf16[2,256,576]{1,2,0:T(8,128)(2,1)}, u32[]{:S(2)}) copy-start(bf16[2,256,576]{1,2,0:T(8,128)(2,1)} %param.10) | copy-start | bytes 1769476
  24.4 31.9 %copy-start.2 = (s32[2]{0:T(128)S(1)}, s32[2]{0:T(128)}, u32[]{:S(2)}) copy-start(s32[2]{0:T(128)} %param.11) | copy-start | bytes 28
  52.8 1.7 %collective-permute-start.4 = (bf16[16,7168]{1,0:T(8,128)(2,1)S(1)}, bf16[16,7168]{1,0:T(8,128)(2,1)S(1)}, u32[]{:S(2)}, u32[]{:S(2)}) collective-permute-start(bf16[16,7168]{1,0:T(8,128)(2,1)S(1)} %get-tuple-element.5), channel_id=1, source_target_pairs={{0,1},{1,0},{2,3},{3,2},{4,5},{5,4},{6,7},{7,6},{8,9},{9,8},{10,11... | collective-permute-start | bytes 688136 | tf_op jit(solution)/shard_map/ppermute | solution.py:230
  54.5 5.5 %collective-permute-start.5 = (bf16[8,7168]{1,0:T(8,128)(2,1)S(1)}, bf16[8,7168]{1,0:T(8,128)(2,1)S(1)}, u32[]{:S(2)}, u32[]{:S(2)}) collective-permute-start(bf16[8,7168]{1,0:T(8,128)(2,1)S(1)} %slice.47), channel_id=1, source_target_pairs={{0,2},{1,3},{2,0},{3,1},{4,6},{5,7},{6,4},{7,5},{8,10},{9,11},{10,... | collective-permute-start | bytes 344072 | tf_op jit(solution)/shard_map/ppermute | solution.py:230
  60.1 4.2 %collective-permute-start.6 = (bf16[4,7168]{1,0:T(4,128)(2,1)S(1)}, bf16[4,7168]{1,0:T(4,128)(2,1)S(1)}, u32[]{:S(2)}, u32[]{:S(2)}) collective-permute-start(bf16[4,7168]{1,0:T(4,128)(2,1)S(1)} %slice.48), channel_id=1, source_target_pairs={{0,4},{1,5},{2,6},{3,7},{4,0},{5,1},{6,2},{7,3},{8,12},{9,13},{10,... | collective-permute-start | bytes 172040 | tf_op jit(solution)/shard_map/ppermute | solution.py:230
  64.4 4.8 %collective-permute-start.7 = (bf16[2,7168]{1,0:T(2,128)(2,1)S(1)}, bf16[2,7168]{1,0:T(2,128)(2,1)S(1)}, u32[]{:S(2)}, u32[]{:S(2)}) collective-permute-start(bf16[2,7168]{1,0:T(2,128)(2,1)S(1)} %slice.49), channel_id=1, source_target_pairs={{0,8},{1,9},{2,10},{3,11},{4,12},{5,13},{6,14},{7,15},{8,0},{9,1},... | collective-permute-start | bytes 86024 | tf_op jit(solution)/shard_map/ppermute | solution.py:230
